TPU v7x, 128 devices: a whole 4x4x4 slice. The times are simulated.
128 devices in a mesh: wide: 16 (over z, y), narrow: 8 (over x, core).
Axes of the slice: x: 4, y: 4, z: 4, core: 2. Of those that a mesh axis runs over, the one named last changes fastest.
Arguments:
- hidden_in: bfloat16 [2048, 2048], P('wide'), may hold values from -6 to 6
- attn_gain: float32 [2048], replicated, may hold values from 0.1 to 1.9
- w_qkv: bfloat16 [2048, 4096], P('wide', 'narrow'), may hold values from -0.125 to 0.125
- q_gain: float32 [128], replicated, may hold values from 0.5 to 10
- k_gain: float32 [128], replicated, may hold values from 0.1 to 1.9
- w_out: bfloat16 [2048, 2048], P('narrow', 'wide'), may hold values from -0.125 to 0.125
- prefix_cache: bfloat16 [2, 64, 4096, 1024], P(None, 'wide', None, 'narrow'), may hold values from -150 to 150
- tail_cache: bfloat16 [2, 1024, 256, 1024], P(None, 'wide', None, 'narrow'), may hold values from -150 to 150
- prompt_lens: int32 [64], replicated, may hold values from 1 to 4096
- tail_lens: int32 [1024], P('wide'), may hold values from 1 to 256
- slot_prompt: int32 [64], replicated, may hold values from 0 to 63, each once
Outputs:
- hidden_out: bfloat16 [2048, 2048], P('wide')
- scores: float32 [2048, 16], P('wide', 'narrow')
- new_cache: bfloat16 [2, 2048, 1024], P(None, 'wide', 'narrow')
Inputs may be any that keep to these rules, and one draw needn't show every extreme that they name: `slot_prompt`: each prompt is held in exactly one slot.
All inputs are finite; a program needn't handle non-finite values.
Results may differ from a plain program's by a relative error of at most 0.007.
Values may be sent and summed in bfloat16 or wider, within the bound.
No kernel may reach another device: no remote copies, remote signals or barrier semaphores. Data moves between devices by JAX's collectives and lax.ppermute only.
A program may use at most 128 MiB of HBM per device.

v0:
```python
import math
import jax
import jax.numpy as jnp
from jax import lax
from jax.sharding import PartitionSpec as P

HEADS = 16
KVH = 8
HD = 128
CONT = 16
NEW = 2
PLEN = 4096
TLEN = 256
epsilon = 1e-06
rope_base = 1000000.0
negative_fill = -1e30


def rms_norm(values, norm_gain):
    mean_square = jnp.mean(values * values, axis=-1, keepdims=True)
    return values * lax.rsqrt(mean_square + epsilon) * norm_gain


def rotate(values, position):
    half_width = values.shape[-1] // 2
    channel = jnp.arange(half_width, dtype=jnp.float32)
    inverse_freq = jnp.exp(channel * (-2.0 / values.shape[-1]) * math.log(rope_base))
    angles = position[..., None] * inverse_freq
    cosine = jnp.cos(angles)
    sines = jnp.sin(angles)
    leading = values[..., :half_width]
    trailing = values[..., half_width:]
    return jnp.concatenate(
        [leading * cosine - trailing * sines, trailing * cosine + leading * sines], axis=-1
    )


def lookup(indices, lookup_table):
    entries = jnp.arange(lookup_table.shape[0], dtype=jnp.int32)
    return jnp.sum(
        jnp.where(indices[:, None] == entries[None, :], lookup_table[None, :], 0), axis=1
    )


def combine_parts(prefix_out, prefix_lse, tail_out, tail_lse):
    highest = jnp.maximum(prefix_lse, tail_lse)
    prefix_share = jnp.exp(prefix_lse - highest)
    tail_share = jnp.exp(tail_lse - highest)
    merged = (prefix_share[..., None] * prefix_out + tail_share[..., None] * tail_out) / (
        prefix_share + tail_share
    )[..., None]
    return (merged.astype(jnp.bfloat16), highest + jnp.log(prefix_share + tail_share))


def body(
    hidden_in,
    attn_gain,
    w_qkv,
    q_gain,
    k_gain,
    w_out,
    prefix_cache,
    tail_cache,
    prompt_lens,
    tail_lens,
    slot_prompt,
):
    group_size = HEADS // KVH
    per_prompt = CONT * NEW
    scaling = HD ** (-0.5)
    wide_index = lax.axis_index("wide")
    rows_dev = hidden_in.shape[0]
    conts_dev = tail_cache.shape[1]
    slot_count = prefix_cache.shape[1]
    groups = prefix_cache.shape[3] // HD
    heads_dev = groups * group_size
    residual = hidden_in.astype(jnp.float32)
    normed = rms_norm(residual, attn_gain).astype(jnp.bfloat16)
    regrouped = lax.all_to_all(normed, "wide", split_axis=1, concat_axis=0, tiled=True)
    projected = lax.psum_scatter(
        jnp.dot(regrouped, w_qkv, preferred_element_type=jnp.float32),
        "wide",
        scatter_dimension=0,
        tiled=True,
    )
    projected = projected.reshape(rows_dev, groups, group_size + 2, HD)
    row_index = wide_index * rows_dev + jnp.arange(rows_dev, dtype=jnp.int32)
    continuation = row_index // NEW
    prompt_index = continuation // CONT
    step_index = row_index % NEW
    local_cont = continuation - wide_index * conts_dev
    position = (
        lookup(prompt_index, prompt_lens) + lookup(local_cont, tail_lens) + step_index
    ).astype(jnp.float32)
    queries = rotate(
        rms_norm(projected[:, :, :group_size], q_gain), position[:, None, None]
    ).astype(jnp.bfloat16)
    new_keys = rotate(rms_norm(projected[:, :, group_size], k_gain), position[:, None]).astype(
        jnp.bfloat16
    )
    new_values = projected[:, :, group_size + 1].astype(jnp.bfloat16)
    everyone = lax.all_gather(queries.reshape(rows_dev, heads_dev * HD), "wide", axis=0, tiled=True)
    global_slot = wide_index * slot_count + jnp.arange(slot_count, dtype=jnp.int32)
    owners = lookup(global_slot, slot_prompt)
    slot_length = lookup(owners, prompt_lens)
    first_row = owners * per_prompt
    chosen = jax.vmap(
        lambda row_begin: lax.dynamic_slice_in_dim(everyone, row_begin, per_prompt, 0)
    )(first_row)
    chosen = chosen.reshape(slot_count, per_prompt, groups, group_size, HD)
    held_keys = prefix_cache[0].reshape(slot_count, PLEN, groups, HD)
    held_values = prefix_cache[1].reshape(slot_count, PLEN, groups, HD)
    prefix_scores = (
        jnp.einsum("srghd,skgd->srghk", chosen, held_keys, preferred_element_type=jnp.float32)
        * scaling
    )
    alive = jnp.arange(PLEN, dtype=jnp.int32)[None, :] < slot_length[:, None]
    prefix_scores = jnp.where(alive[:, None, None, None, :], prefix_scores, negative_fill)
    prefix_max = jnp.max(prefix_scores, axis=-1)
    prefix_weights = jnp.exp(prefix_scores - prefix_max[..., None])
    prefix_total = jnp.sum(prefix_weights, axis=-1)
    prefix_num = jnp.einsum(
        "srghk,skgd->srghd",
        prefix_weights.astype(jnp.bfloat16),
        held_values,
        preferred_element_type=jnp.float32,
    )
    prefix_out = prefix_num / prefix_total[..., None]
    prefix_lse = prefix_max + jnp.log(prefix_total)
    spread_out = jnp.zeros((everyone.shape[0], heads_dev * HD), jnp.float32)
    spread_lse = jnp.zeros((everyone.shape[0], heads_dev), jnp.float32)
    for slot_number in range(slot_count):
        spread_out = lax.dynamic_update_slice_in_dim(
            spread_out,
            prefix_out[slot_number].reshape(per_prompt, heads_dev * HD),
            first_row[slot_number],
            0,
        )
        spread_lse = lax.dynamic_update_slice_in_dim(
            spread_lse,
            prefix_lse[slot_number].reshape(per_prompt, heads_dev),
            first_row[slot_number],
            0,
        )
    mine_out, mine_lse = (
        lax.psum_scatter(spread_out, "wide", scatter_dimension=0, tiled=True),
        lax.psum_scatter(spread_lse, "wide", scatter_dimension=0, tiled=True),
    )
    tail_query = queries.reshape(conts_dev, NEW, groups, group_size, HD)
    tail_keys = tail_cache[0].reshape(conts_dev, TLEN, groups, HD)
    tail_values = tail_cache[1].reshape(conts_dev, TLEN, groups, HD)
    own_keys = new_keys.reshape(conts_dev, NEW, groups, HD)
    own_values = new_values.reshape(conts_dev, NEW, groups, HD)
    cached_scores = (
        jnp.einsum("ctghd,csgd->ctghs", tail_query, tail_keys, preferred_element_type=jnp.float32)
        * scaling
    )
    cached_alive = jnp.arange(TLEN, dtype=jnp.int32)[None, :] < tail_lens[:, None]
    cached_scores = jnp.where(cached_alive[:, None, None, None, :], cached_scores, negative_fill)
    own_scores = (
        jnp.einsum("ctghd,cugd->ctghu", tail_query, own_keys, preferred_element_type=jnp.float32)
        * scaling
    )
    causal = jnp.arange(NEW)[None, :] <= jnp.arange(NEW)[:, None]
    own_scores = jnp.where(causal[None, :, None, None, :], own_scores, negative_fill)
    tail_max = jnp.maximum(jnp.max(cached_scores, axis=-1), jnp.max(own_scores, axis=-1))
    cached_weights = jnp.exp(cached_scores - tail_max[..., None])
    own_weights = jnp.exp(own_scores - tail_max[..., None])
    tail_total = jnp.sum(cached_weights, axis=-1) + jnp.sum(own_weights, axis=-1)
    tail_num = jnp.einsum(
        "ctghs,csgd->ctghd",
        cached_weights.astype(jnp.bfloat16),
        tail_values,
        preferred_element_type=jnp.float32,
    )
    tail_num = tail_num + jnp.einsum(
        "ctghu,cugd->ctghd",
        own_weights.astype(jnp.bfloat16),
        own_values,
        preferred_element_type=jnp.float32,
    )
    tail_out = (tail_num / tail_total[..., None]).reshape(rows_dev, heads_dev, HD)
    tail_lse = (tail_max + jnp.log(tail_total)).reshape(rows_dev, heads_dev)
    attention, scores = combine_parts(
        mine_out.reshape(rows_dev, heads_dev, HD), mine_lse, tail_out, tail_lse
    )
    attention = attention.reshape(rows_dev, heads_dev * HD)
    partial_out = jnp.dot(
        attention,
        lax.all_gather(w_out, "wide", axis=1, tiled=True),
        preferred_element_type=jnp.float32,
    )
    summed = lax.psum(partial_out.astype(jnp.bfloat16), "narrow").astype(jnp.float32)
    hidden_out = (residual + summed).astype(jnp.bfloat16)
    new_cache = jnp.stack(
        [new_keys.reshape(rows_dev, groups * HD), new_values.reshape(rows_dev, groups * HD)]
    )
    return (hidden_out, scores, new_cache)


def solution(mesh):
    in_specs = (
        P("wide", None),
        P(),
        P("wide", "narrow"),
        P(),
        P(),
        P("narrow", "wide"),
        P(None, "wide", None, "narrow"),
        P(None, "wide", None, "narrow"),
        P(),
        P("wide"),
        P(),
    )
    out_specs = (P("wide", None), P("wide", "narrow"), P(None, "wide", "narrow"))
    return jax.shard_map(body, mesh=mesh, in_specs=in_specs, out_specs=out_specs, check_vma=False)
```

profile of v0, /device:TPU:0, one launch (start us, length us, event | category | flops | bytes accessed | tf_op | source)
XLA Modules:
  0.0 435.0 jit_solution(1047986188421033371)
XLA Ops:
  8.5 1.3 copy_bitcast_fusion
  9.8 19.5 %all_to_all.19 = bf16[128,16,128]{2,0,1:T(8,128)(2,1)S(1)} all-to-all(bf16[128,16,128]{2,0,1:T(8,128)(2,1)S(1)} %copy_bitcast_fusion), channel_id=1, replica_groups=mesh['wide'=16,'narrow'=8] {'wide'}, dimensions={1} | all-to-all | bytes 1048576 | tf_op jit(solution)/shard_map/all_to_all | solution.py:79
  29.3 2.6 fusion.99
  32.5 74.9 %reduce-scatter.6.cloned.1.call-done = f32[128,512]{1,0:T(8,128)} async-done(((f32[2048,512]{1,0:T(8,128)}), f32[128,512]{1,0:T(8,128)}) %reduce-scatter.6.cloned.1.call-update) | async-done | bytes 262160 | tf_op jit(solution)/shard_map/reduce_scatter | solution.py:80
  118.9 33.5 %all-gather.3.cloned.1.call-done = bf16[2048,256]{1,0:T(8,128)(2,1)} async-done(((bf16[128,256]{1,0:T(8,128)(2,1)}), bf16[2048,256]{1,0:T(8,128)(2,1)}) %all-gather.3.cloned.1.call-update) | async-done | bytes 1048592 | tf_op jit(solution)/shard_map/all_gather | solution.py:102
  152.4 7.9 %while.1 = (s32[]{:T(128)}, bf16[2048,256]{1,0:T(8,128)(2,1)}, s32[4,2]{0,1:T(2,128)S(1)}, bf16[4,32,256]{2,1,0:T(8,128)(2,1)S(1)}, s32[]{:T(128)}) while((s32[]{:T(128)}, bf16[2048,256]{1,0:T(8,128)(2,1)}, s32[4,2]{0,1:T(2,128)S(1)}, bf16[4,32,256]{2,1,0:T(8,128)(2,1)S(1)}, s32[]{:T(128)}) %tuple.42), condition=%wide.while_cond, body=%wide.while_body.sunk | while | flops 2 | bytes 32865 | solution.py:108
  153.0 1.4 bitcast_dynamic-update-slice_fusion.2
  155.0 1.4 bitcast_dynamic-update-slice_fusion.2
  157.0 1.4 bitcast_dynamic-update-slice_fusion.2
  159.0 1.4 bitcast_dynamic-update-slice_fusion.2
  160.3 3.9 fusion.96
  164.2 1.9 copy-done.1
  167.8 1.4 copy.100
  169.9 4.5 %fusion.45 = f32[4,32,1,2,128]{4,1,3,0,2:T(8,128)S(1)} fusion(bf16[2,4,4096,128]{3,2,1,0:T(8,128)(2,1)} %param.17, f32[4,32,1,2,4096]{4,1,3,0,2:T(8,128)} %copy-done.1, f32[4,32,2]{1,2,0:T(2,128)S(1)} %get-tuple-element.45, f32[4,32,2]{1,2,0:T(2,128)S(1)} %fusion.15), kind=kOutput, calls=%fused_computation.35 | convolution fusion | flops 270565376 | bytes 8521728 | tf_op jit(solution)/shard_map/srghk,skgd->srghd/dot_general | solution.py:122
  176.1 1.3 copy-done.2
  178.5 1.4 fusion.98
  179.9 3.6 fusion.97
  184.6 3.0 fusion.61
  187.7 54.0 %reduce-scatter.10.cloned.1.call-done = f32[128,2]{1,0:T(8,128)} async-done(((f32[2048,2]{1,0:T(8,128)}), f32[128,2]{1,0:T(8,128)}) %reduce-scatter.10.cloned.1.call-update) | async-done | bytes 1040
  243.5 42.9 %all-gather.5.cloned.1.call-done = bf16[256,2048]{1,0:T(8,128)(2,1)} async-done(((bf16[256,128]{1,0:T(8,128)(2,1)}), bf16[256,2048]{1,0:T(8,128)(2,1)}) %all-gather.5.cloned.1.call-update) | async-done | bytes 1048592 | tf_op jit(solution)/shard_map/all_gather | solution.py:190
  286.4 76.9 %reduce-scatter.8.cloned.1.call-done = f32[128,256]{1,0:T(8,128)} async-done(((f32[2048,256]{1,0:T(8,128)}), f32[128,256]{1,0:T(8,128)}) %reduce-scatter.8.cloned.1.call-update) | async-done | bytes 131088 | tf_op jit(solution)/shard_map/reduce_scatter | solution.py:146
  363.8 2.4 convolution_convert_fusion
  367.0 59.2 %all-reduce.3.cloned.1.call-done = bf16[128,2048]{1,0:T(8,128)(2,1)} async-done(((bf16[128,2048]{1,0:T(8,128)(2,1)}), bf16[128,2048]{1,0:T(8,128)(2,1)}) %all-reduce.3.cloned.1.call-update) | async-done | bytes 524304 | tf_op jit(solution)/shard_map/psum | solution.py:193
  426.2 2.0 fusion.54
  (106 shorter events, 17.3 us)
Async XLA Ops:
  7.2 22.1 %copy-start = (bf16[128,512]{1,0:T(8,128)(2,1)S(1)}, bf16[128,512]{1,0:T(8,128)(2,1)}, u32[]{:S(2)}) copy-start(bf16[128,512]{1,0:T(8,128)(2,1)} %param.13) | copy-start | bytes 393220
  7.2 100.2 %reduce-scatter.6.cloned.1.call-start = ((), (), s32[]{:S(2)}) async-start(), calls=%async_computation.4 | async-start | bytes 4456448 | tf_op jit(solution)/shard_map/reduce_scatter | solution.py:80
  29.2 2.7 copy-start.6
  29.3 2.8 copy-start.8
  29.3 79.4 %copy-start.4 = (f32[128]{0:T(128)S(1)}, f32[128]{0:T(128)}, u32[]{:S(2)}) copy-start(f32[128]{0:T(128)} %param.14) | copy-start | bytes 1540
  31.9 78.3 %copy-start.7 = (s32[64]{0:T(128)S(1)}, s32[64]{0:T(128)}, u32[]{:S(2)}) copy-start(s32[64]{0:T(128)} %param.21) | copy-start | bytes 772
  31.9 120.6 %all-gather.3.cloned.1.call-start = ((), (), s32[]{:S(2)}) async-start(), calls=%async_computation.5 | async-start | bytes 1114112 | tf_op jit(solution)/shard_map/all_gather | solution.py:102
  110.1 131.6 %reduce-scatter.10.cloned.1.call-start = ((), (), s32[]{:S(2)}) async-start(), calls=%async_computation.9 | async-start | bytes 1114112
  164.2 1.9 copy-start.1
  169.2 117.1 %all-gather.5.cloned.1.call-start = ((), (), s32[]{:S(2)}) async-start(), calls=%async_computation.7 | async-start | bytes 1114112 | tf_op jit(solution)/shard_map/all_gather | solution.py:190
  169.8 193.4 %reduce-scatter.8.cloned.1.call-start = ((), (), s32[]{:S(2)}) async-start(), calls=%async_computation.6 | async-start | bytes 2228224 | tf_op jit(solution)/shard_map/reduce_scatter | solution.py:146
  174.4 3.7 copy-start.5
  176.1 1.4 copy-start.2
  177.5 248.7 %all-reduce.3.cloned.1.call-start = ((), (), s32[]{:S(2)}) async-start(), calls=%async_computation.8 | async-start | bytes 1048576 | tf_op jit(solution)/shard_map/psum | solution.py:193
  184.6 241.6 %copy-start.3 = (bf16[128,2048]{1,0:T(8,128)(2,1)S(1)}, bf16[128,2048]{1,0:T(8,128)(2,1)}, u32[]{:S(2)}) copy-start(bf16[128,2048]{1,0:T(8,128)(2,1)} %param.11) | copy-start | bytes 1572868
Sparse Core Ops, SparseCore 0:
  32.0 75.3 reduce-scatter.5
  110.4 42.0 all-gather.2
  169.4 72.2 reduce-scatter.9
  243.6 42.6 all-gather.4
  289.5 73.7 reduce-scatter.7
  366.4 59.7 all-reduce.2
where the time goes:
time: 436 us; the launch traced here: 435 us
  waiting for transfers between devices  342 us (78%)
  between operations  22.1 us (5%)
  matrix products  21.7 us (5%)
  local copies, waits for them, and re-layouts  19.5 us (4%)
  blocking collectives  19.5 us (4%)
  other arithmetic  9.84 us (2%)
    reduce_scatter x1, waiting for transfers between devices, body(): lax.psum_scatter(spread_out, 'wide', scatter_dimension=0, tiled=True)  76.9 us
    reduce_scatter x1, waiting for transfers between devices, body(): lax.psum_scatter(jnp.dot(regrouped, w_qkv, preferred_element_type=jnp.flo...  74.9 us
    psum x1, waiting for transfers between devices, body(): lax.psum(partial_out.astype(jnp.bfloat16), 'narrow').astype(jnp.float32)  59.2 us
    unnamed x7, waiting for transfers between devices  54.6 us
    all_gather x1, waiting for transfers between devices, body(): lax.all_gather(w_out, 'wide', axis=1, tiled=True)  42.9 us
    all_gather x1, waiting for transfers between devices, body(): lax.all_gather(queries.reshape(rows_dev, heads_dev * HD), 'wide', axis=0,...  33.5 us
    all_to_all x1, blocking collectives, body(): lax.all_to_all(normed, 'wide', split_axis=1, concat_axis=0, tiled=True)  19.5 us
  transfers between devices with their start and end apart: 6, of which 6 were waited for; matrix products, arithmetic and copies ran while one was open for 5% of the time, Pallas kernels for 0%

commit v1 on v0

--- a/solution.py
+++ b/solution.py
@@ -1,3 +1,4 @@
+import functools
 import math
 import jax
 import jax.numpy as jnp
@@ -14,6 +15,33 @@
 epsilon = 1e-06
 rope_base = 1000000.0
 negative_fill = -1e30
+
+
+def review_groups_in(local_x, which_dim):
+    kept_arr = list(local_x.shape[1:])
+    kept_arr[which_dim] *= local_x.shape[0]
+    f_now = jnp.moveaxis(local_x, 0, which_dim).reshape(kept_arr)
+    return f_now
+
+
+def search_inputs_by_axis(original, comm_axis, out_dim):
+    dev_count = lax.axis_size(comm_axis)
+    history = list(map(lambda q: (q, (q + 1) % dev_count), range(dev_count)))
+    mat_out, mid_arr = ([], [])
+    pile = [(k0, hop_no) for hop_no, k0 in history]
+    for ix in range(dev_count - 1):
+        if ix % 2 == 0:
+            mat_out.append(lax.ppermute(mat_out[-1] if mat_out else original, comm_axis, history))
+        else:
+            mid_arr.append(lax.ppermute(mid_arr[-1] if mid_arr else original, comm_axis, pile))
+    taken_in = jnp.stack([*mat_out[::-1], original, *mid_arr], 0)
+    val = lax.axis_index(comm_axis) - len(mat_out)
+    taken_in = taken_in[(jnp.arange(dev_count) - val) % dev_count]
+    plain = review_groups_in(taken_in, out_dim)
+    return plain
+
+
+solve_node = functools.partial(search_inputs_by_axis, comm_axis="wide", out_dim=1)
 
 
 def rms_norm(values, norm_gain):
@@ -185,11 +213,7 @@
         mine_out.reshape(rows_dev, heads_dev, HD), mine_lse, tail_out, tail_lse
     )
     attention = attention.reshape(rows_dev, heads_dev * HD)
-    partial_out = jnp.dot(
-        attention,
-        lax.all_gather(w_out, "wide", axis=1, tiled=True),
-        preferred_element_type=jnp.float32,
-    )
+    partial_out = jnp.dot(attention, solve_node(w_out), preferred_element_type=jnp.float32)
     summed = lax.psum(partial_out.astype(jnp.bfloat16), "narrow").astype(jnp.float32)
     hidden_out = (residual + summed).astype(jnp.bfloat16)
     new_cache = jnp.stack(

time: 436 us -> 393 us (0.901)
  waiting for transfers between devices: 342 us -> 249 us
  starting transfers between devices: 0.42 us -> 39.3 us
  local copies, waits for them, and re-layouts: 19.5 us -> 28 us
    reduce_scatter x1, waiting for transfers between devices: 74.9 us -> 5.9 us  [body(): lax.psum_scatter(jnp.dot(regrouped, w_qkv, preferred_element_type=jnp.flo...]
    all_gather x1 -> x0, waiting for transfers between devices: 42.9 us -> none  [body(): lax.all_gather(w_out, 'wide', axis=1, tiled=True)]
    ppermute x0 -> x15, starting transfers between devices: none -> 38.9 us  [the longest x7 38.3 us: search_inputs_by_axis(): lax.ppermute(mid_arr[-1] if mid_arr else original, comm_axis, pile)]
    ppermute x0 -> x15, waiting for transfers between devices: none -> 21.1 us  [the longest x8 16.4 us: search_inputs_by_axis(): lax.ppermute(mat_out[-1] if mat_out else original, comm_axis, history)]
    all_gather x1, waiting for transfers between devices: 33.5 us -> 41.8 us  [body(): lax.all_gather(queries.reshape(rows_dev, heads_dev * HD), 'wide', axis=0,...]
    unnamed x7 -> x6, waiting for transfers between devices: 54.6 us -> 46.5 us
    unnamed x25 -> x52, local copies, waits for them, and re-layouts: 6.26 us -> 10.3 us
  transfers between devices with their start and end apart: 6 -> 20, of which waited for: 6 -> 12; matrix products, arithmetic and copies ran while one was open for 5% -> 13% of each run, Pallas kernels for 0% -> 0%
where the time goes in v1:
time: 393 us; the launch traced here: 392 us
  waiting for transfers between devices  249 us (63%)
  starting transfers between devices  39.3 us (10%)
  local copies, waits for them, and re-layouts  28 us (7%)
  between operations  22.1 us (6%)
  matrix products  21.2 us (5%)
  blocking collectives  19.5 us (5%)
  other arithmetic  12.3 us (3%)
    reduce_scatter x1, waiting for transfers between devices, body(): lax.psum_scatter(spread_out, 'wide', scatter_dimension=0, tiled=True)  75.1 us
    psum x1, waiting for transfers between devices, body(): lax.psum(partial_out.astype(jnp.bfloat16), 'narrow').astype(jnp.float32)  59.1 us
    unnamed x6, waiting for transfers between devices  46.5 us
    all_gather x1, waiting for transfers between devices, body(): lax.all_gather(queries.reshape(rows_dev, heads_dev * HD), 'wide', axis=0,...  41.8 us
    ppermute x7, starting transfers between devices, search_inputs_by_axis(): lax.ppermute(mid_arr[-1] if mid_arr else original, comm_axis, pile)  38.3 us
    all_to_all x1, blocking collectives, body(): lax.all_to_all(normed, 'wide', split_axis=1, concat_axis=0, tiled=True)  19.5 us
    ppermute x8, waiting for transfers between devices, search_inputs_by_axis(): lax.ppermute(mat_out[-1] if mat_out else original, comm_axis, history)  16.4 us
    unnamed x52, local copies, waits for them, and re-layouts  10.3 us
  transfers between devices with their start and end apart: 20, of which 12 were waited for; matrix products, arithmetic and copies ran while one was open for 13% of the time, Pallas kernels for 0%

profile of v1, /device:TPU:0, one launch (start us, length us, event | category | flops | bytes accessed | tf_op | source)
XLA Modules:
  0.0 391.9 jit_solution(2683944788350190424)
XLA Ops:
  9.8 19.5 %all_to_all.19 = bf16[128,16,128]{2,0,1:T(8,128)(2,1)S(1)} all-to-all(bf16[128,16,128]{2,0,1:T(8,128)(2,1)S(1)} %copy_bitcast_fusion), channel_id=1, replica_groups=mesh['wide'=16,'narrow'=8] {'wide'}, dimensions={1} | all-to-all | bytes 1048576 | tf_op jit(solution)/shard_map/all_to_all | solution.py:107
  29.3 2.6 fusion.101
  32.6 4.8 %collective-permute-start.8 = (bf16[256,128]{1,0:T(8,128)(2,1)S(1)}, bf16[256,128]{1,0:T(8,128)(2,1)S(1)}, u32[]{:S(2)}, u32[]{:S(2)}) collective-permute-start(bf16[256,128]{1,0:T(8,128)(2,1)S(1)} %copy-done.5), channel_id=1, source_target_pairs={{8,0},{16,8},{24,16},{32,24},{40,32},{48,40},{56,48},{64,56},{72,6... | collective-permute-start | bytes 196616 | tf_op jit(solution)/shard_map/ppermute | solution.py:36
  39.7 8.2 %collective-permute-done.1 = bf16[256,128]{1,0:T(8,128)(2,1)S(1)} collective-permute-done((bf16[256,128]{1,0:T(8,128)(2,1)S(1)}, bf16[256,128]{1,0:T(8,128)(2,1)S(1)}, u32[]{:S(2)}, u32[]{:S(2)}) %collective-permute-start.1) | collective-permute-done | bytes 65568 | tf_op jit(solution)/shard_map/ppermute | solution.py:34
  47.9 5.3 %collective-permute-start.9 = (bf16[256,128]{1,0:T(8,128)(2,1)S(1)}, bf16[256,128]{1,0:T(8,128)(2,1)S(1)}, u32[]{:S(2)}, u32[]{:S(2)}) collective-permute-start(bf16[256,128]{1,0:T(8,128)(2,1)S(1)} %collective-permute-done.8), channel_id=1, source_target_pairs={{8,0},{16,8},{24,16},{32,24},{40,32},{48,40},{56,48},{64,56},{72,6... | collective-permute-start | bytes 196616 | tf_op jit(solution)/shard_map/ppermute | solution.py:36
  53.3 3.1 collective-permute-done.2
  56.4 5.4 %collective-permute-start.10 = (bf16[256,128]{1,0:T(8,128)(2,1)S(1)}, bf16[256,128]{1,0:T(8,128)(2,1)S(1)}, u32[]{:S(2)}, u32[]{:S(2)}) collective-permute-start(bf16[256,128]{1,0:T(8,128)(2,1)S(1)} %collective-permute-done.9), channel_id=1, source_target_pairs={{8,0},{16,8},{24,16},{32,24},{40,32},{48,40},{56,48},{64,56},{72,6... | collective-permute-start | bytes 196616 | tf_op jit(solution)/shard_map/ppermute | solution.py:36
  61.8 3.9 collective-permute-done.3
  74.2 5.4 %collective-permute-start.11 = (bf16[256,128]{1,0:T(8,128)(2,1)S(1)}, bf16[256,128]{1,0:T(8,128)(2,1)S(1)}, u32[]{:S(2)}, u32[]{:S(2)}) collective-permute-start(bf16[256,128]{1,0:T(8,128)(2,1)S(1)} %collective-permute-done.10), channel_id=1, source_target_pairs={{8,0},{16,8},{24,16},{32,24},{40,32},{48,40},{56,48},{64,56},{72,6... | collective-permute-start | bytes 196616 | tf_op jit(solution)/shard_map/ppermute | solution.py:36
  81.7 5.8 %collective-permute-start.12 = (bf16[256,128]{1,0:T(8,128)(2,1)S(1)}, bf16[256,128]{1,0:T(8,128)(2,1)S(1)}, u32[]{:S(2)}, u32[]{:S(2)}) collective-permute-start(bf16[256,128]{1,0:T(8,128)(2,1)S(1)} %collective-permute-done.11), channel_id=1, source_target_pairs={{8,0},{16,8},{24,16},{32,24},{40,32},{48,40},{56,48},{64,56},{72,6... | collective-permute-start | bytes 196616 | tf_op jit(solution)/shard_map/ppermute | solution.py:36
  89.4 5.7 %collective-permute-start.13 = (bf16[256,128]{1,0:T(8,128)(2,1)S(1)}, bf16[256,128]{1,0:T(8,128)(2,1)}, u32[]{:S(2)}, u32[]{:S(2)}) collective-permute-start(bf16[256,128]{1,0:T(8,128)(2,1)S(1)} %collective-permute-done.12), channel_id=1, source_target_pairs={{8,0},{16,8},{24,16},{32,24},{40,32},{48,40},{56,48},{64,56},{72,6... | collective-permute-start | bytes 196616 | tf_op jit(solution)/shard_map/ppermute | solution.py:36
  97.0 5.9 %collective-permute-start.14 = (bf16[256,128]{1,0:T(8,128)(2,1)}, bf16[256,128]{1,0:T(8,128)(2,1)}, u32[]{:S(2)}, u32[]{:S(2)}) collective-permute-start(bf16[256,128]{1,0:T(8,128)(2,1)} %collective-permute-done.13), channel_id=1, source_target_pairs={{8,0},{16,8},{24,16},{32,24},{40,32},{48,40},{56,48},{64,56},{72,6... | collective-permute-start | bytes 196616 | tf_op jit(solution)/shard_map/ppermute | solution.py:36
  102.9 5.9 %reduce-scatter.6.cloned.1.call-done = f32[128,512]{1,0:T(8,128)} async-done(((f32[2048,512]{1,0:T(8,128)}), f32[128,512]{1,0:T(8,128)}) %reduce-scatter.6.cloned.1.call-update) | async-done | bytes 262160 | tf_op jit(solution)/shard_map/reduce_scatter | solution.py:108
  111.9 41.8 %all-gather.2.cloned.1.call-done = bf16[2048,256]{1,0:T(8,128)(2,1)} async-done(((bf16[128,256]{1,0:T(8,128)(2,1)}), bf16[2048,256]{1,0:T(8,128)(2,1)}) %all-gather.2.cloned.1.call-update) | async-done | bytes 1048592 | tf_op jit(solution)/shard_map/all_gather | solution.py:130
  153.7 7.5 %while.1 = (s32[]{:T(128)}, bf16[2048,256]{1,0:T(8,128)(2,1)}, s32[4,2]{0,1:T(2,128)S(1)}, bf16[4,32,256]{2,1,0:T(8,128)(2,1)S(1)}, s32[]{:T(128)}) while((s32[]{:T(128)}, bf16[2048,256]{1,0:T(8,128)(2,1)}, s32[4,2]{0,1:T(2,128)S(1)}, bf16[4,32,256]{2,1,0:T(8,128)(2,1)S(1)}, s32[]{:T(128)}) %tuple.42), condition=%wide.while_cond, body=%wide.while_body.sunk | while | flops 2 | bytes 32865 | solution.py:136
  161.2 3.8 fusion.98
  165.8 3.3 fusion.45
  187.3 2.3 fusion.100
  189.6 3.6 fusion.99
  194.4 3.0 fusion.61
  197.4 46.5 %reduce-scatter.10.cloned.1.call-done = f32[128,2]{1,0:T(8,128)} async-done(((f32[2048,2]{1,0:T(8,128)}), f32[128,2]{1,0:T(8,128)}) %reduce-scatter.10.cloned.1.call-update) | async-done | bytes 1040
  245.7 75.1 %reduce-scatter.8.cloned.1.call-done = f32[128,256]{1,0:T(8,128)} async-done(((f32[2048,256]{1,0:T(8,128)}), f32[128,256]{1,0:T(8,128)}) %reduce-scatter.8.cloned.1.call-update) | async-done | bytes 131088 | tf_op jit(solution)/shard_map/reduce_scatter | solution.py:174
  321.4 2.2 convolution_convert_fusion
  324.3 59.1 %all-reduce.3.cloned.1.call-done = bf16[128,2048]{1,0:T(8,128)(2,1)} async-done(((bf16[128,2048]{1,0:T(8,128)(2,1)}), bf16[128,2048]{1,0:T(8,128)(2,1)}) %all-reduce.3.cloned.1.call-update) | async-done | bytes 524304 | tf_op jit(solution)/shard_map/psum | solution.py:217
  (165 shorter events, 47.7 us)
Async XLA Ops:
  7.2 22.1 %copy-start = (bf16[128,512]{1,0:T(8,128)(2,1)S(1)}, bf16[128,512]{1,0:T(8,128)(2,1)}, u32[]{:S(2)}) copy-start(bf16[128,512]{1,0:T(8,128)(2,1)} %param.13) | copy-start | bytes 393220
  7.2 101.6 %reduce-scatter.6.cloned.1.call-start = ((), (), s32[]{:S(2)}) async-start(), calls=%async_computation.4 | async-start | bytes 4456448 | tf_op jit(solution)/shard_map/reduce_scatter | solution.py:108
  29.3 80.8 %copy-start.11 = (f32[128]{0:T(128)S(1)}, f32[128]{0:T(128)}, u32[]{:S(2)}) copy-start(f32[128]{0:T(128)} %param.14) | copy-start | bytes 1540
  31.9 121.8 %all-gather.2.cloned.1.call-start = ((), (), s32[]{:S(2)}) async-start(), calls=%async_computation.5 | async-start | bytes 1114112 | tf_op jit(solution)/shard_map/all_gather | solution.py:130
  32.0 7.7 %collective-permute-start = (bf16[256,128]{1,0:T(8,128)(2,1)S(1)}, bf16[256,128]{1,0:T(8,128)(2,1)S(1)}, u32[]{:S(2)}, u32[]{:S(2)}) collective-permute-start(bf16[256,128]{1,0:T(8,128)(2,1)S(1)} %copy-done.5), channel_id=1, source_target_pairs={{0,8},{8,16},{16,24},{24,32},{32,40},{40,48},{48,56},{56,64},{64,7... | collective-permute-start | bytes 196616 | tf_op jit(solution)/shard_map/ppermute | solution.py:34
  32.6 15.3 %collective-permute-start.8 = (bf16[256,128]{1,0:T(8,128)(2,1)S(1)}, bf16[256,128]{1,0:T(8,128)(2,1)S(1)}, u32[]{:S(2)}, u32[]{:S(2)}) collective-permute-start(bf16[256,128]{1,0:T(8,128)(2,1)S(1)} %copy-done.5), channel_id=1, source_target_pairs={{8,0},{16,8},{24,16},{32,24},{40,32},{48,40},{56,48},{64,56},{72,6... | collective-permute-start | bytes 196616 | tf_op jit(solution)/shard_map/ppermute | solution.py:36
  39.6 8.3 %collective-permute-start.1 = (bf16[256,128]{1,0:T(8,128)(2,1)S(1)}, bf16[256,128]{1,0:T(8,128)(2,1)S(1)}, u32[]{:S(2)}, u32[]{:S(2)}) collective-permute-start(bf16[256,128]{1,0:T(8,128)(2,1)S(1)} %collective-permute-done), channel_id=1, source_target_pairs={{0,8},{8,16},{16,24},{24,32},{32,40},{40,48},{48,56},{56,64},{64,7... | collective-permute-start | bytes 196616 | tf_op jit(solution)/shard_map/ppermute | solution.py:34
  47.9 8.4 %collective-permute-start.2 = (bf16[256,128]{1,0:T(8,128)(2,1)S(1)}, bf16[256,128]{1,0:T(8,128)(2,1)S(1)}, u32[]{:S(2)}, u32[]{:S(2)}) collective-permute-start(bf16[256,128]{1,0:T(8,128)(2,1)S(1)} %collective-permute-done.1), channel_id=1, source_target_pairs={{0,8},{8,16},{16,24},{24,32},{32,40},{40,48},{48,56},{56,64},{64,7... | collective-permute-start | bytes 196616 | tf_op jit(solution)/shard_map/ppermute | solution.py:34
  47.9 8.5 %collective-permute-start.9 = (bf16[256,128]{1,0:T(8,128)(2,1)S(1)}, bf16[256,128]{1,0:T(8,128)(2,1)S(1)}, u32[]{:S(2)}, u32[]{:S(2)}) collective-permute-start(bf16[256,128]{1,0:T(8,128)(2,1)S(1)} %collective-permute-done.8), channel_id=1, source_target_pairs={{8,0},{16,8},{24,16},{32,24},{40,32},{48,40},{56,48},{64,56},{72,6... | collective-permute-start | bytes 196616 | tf_op jit(solution)/shard_map/ppermute | solution.py:36
  56.4 9.3 %collective-permute-start.3 = (bf16[256,128]{1,0:T(8,128)(2,1)S(1)}, bf16[256,128]{1,0:T(8,128)(2,1)S(1)}, u32[]{:S(2)}, u32[]{:S(2)}) collective-permute-start(bf16[256,128]{1,0:T(8,128)(2,1)S(1)} %collective-permute-done.2), channel_id=1, source_target_pairs={{0,8},{8,16},{16,24},{24,32},{32,40},{40,48},{48,56},{56,64},{64,7... | collective-permute-start | bytes 196616 | tf_op jit(solution)/shard_map/ppermute | solution.py:34
  56.4 17.7 %collective-permute-start.10 = (bf16[256,128]{1,0:T(8,128)(2,1)S(1)}, bf16[256,128]{1,0:T(8,128)(2,1)S(1)}, u32[]{:S(2)}, u32[]{:S(2)}) collective-permute-start(bf16[256,128]{1,0:T(8,128)(2,1)S(1)} %collective-permute-done.9), channel_id=1, source_target_pairs={{8,0},{16,8},{24,16},{32,24},{40,32},{48,40},{56,48},{64,56},{72,6... | collective-permute-start | bytes 196616 | tf_op jit(solution)/shard_map/ppermute | solution.py:36
  65.7 13.9 %collective-permute-start.4 = (bf16[256,128]{1,0:T(8,128)(2,1)S(1)}, bf16[256,128]{1,0:T(8,128)(2,1)S(1)}, u32[]{:S(2)}, u32[]{:S(2)}) collective-permute-start(bf16[256,128]{1,0:T(8,128)(2,1)S(1)} %collective-permute-done.3), channel_id=1, source_target_pairs={{0,8},{8,16},{16,24},{24,32},{32,40},{40,48},{48,56},{56,64},{64,7... | collective-permute-start | bytes 196616 | tf_op jit(solution)/shard_map/ppermute | solution.py:34
  74.1 28.7 %copy-start.6 = (bf16[256,128]{1,0:T(8,128)(2,1)}, bf16[256,128]{1,0:T(8,128)(2,1)S(1)}, u32[]{:S(2)}) copy-start(bf16[256,128]{1,0:T(8,128)(2,1)S(1)} %collective-permute-done.10) | copy-start | bytes 196612
  74.2 7.5 %collective-permute-start.11 = (bf16[256,128]{1,0:T(8,128)(2,1)S(1)}, bf16[256,128]{1,0:T(8,128)(2,1)S(1)}, u32[]{:S(2)}, u32[]{:S(2)}) collective-permute-start(bf16[256,128]{1,0:T(8,128)(2,1)S(1)} %collective-permute-done.10), channel_id=1, source_target_pairs={{8,0},{16,8},{24,16},{32,24},{40,32},{48,40},{56,48},{64,56},{72,6... | collective-permute-start | bytes 196616 | tf_op jit(solution)/shard_map/ppermute | solution.py:36
  79.6 7.9 %collective-permute-start.5 = (bf16[256,128]{1,0:T(8,128)(2,1)S(1)}, bf16[256,128]{1,0:T(8,128)(2,1)S(1)}, u32[]{:S(2)}, u32[]{:S(2)}) collective-permute-start(bf16[256,128]{1,0:T(8,128)(2,1)S(1)} %collective-permute-done.4), channel_id=1, source_target_pairs={{0,8},{8,16},{16,24},{24,32},{32,40},{40,48},{48,56},{56,64},{64,7... | collective-permute-start | bytes 196616 | tf_op jit(solution)/shard_map/ppermute | solution.py:34
  81.7 7.7 %collective-permute-start.12 = (bf16[256,128]{1,0:T(8,128)(2,1)S(1)}, bf16[256,128]{1,0:T(8,128)(2,1)S(1)}, u32[]{:S(2)}, u32[]{:S(2)}) collective-permute-start(bf16[256,128]{1,0:T(8,128)(2,1)S(1)} %collective-permute-done.11), channel_id=1, source_target_pairs={{8,0},{16,8},{24,16},{32,24},{40,32},{48,40},{56,48},{64,56},{72,6... | collective-permute-start | bytes 196616 | tf_op jit(solution)/shard_map/ppermute | solution.py:36
  87.5 7.6 %collective-permute-start.6 = (bf16[256,128]{1,0:T(8,128)(2,1)S(1)}, bf16[256,128]{1,0:T(8,128)(2,1)S(1)}, u32[]{:S(2)}, u32[]{:S(2)}) collective-permute-start(bf16[256,128]{1,0:T(8,128)(2,1)S(1)} %collective-permute-done.5), channel_id=1, source_target_pairs={{0,8},{8,16},{16,24},{24,32},{32,40},{40,48},{48,56},{56,64},{64,7... | collective-permute-start | bytes 196616 | tf_op jit(solution)/shard_map/ppermute | solution.py:34
  89.4 7.6 %collective-permute-start.13 = (bf16[256,128]{1,0:T(8,128)(2,1)S(1)}, bf16[256,128]{1,0:T(8,128)(2,1)}, u32[]{:S(2)}, u32[]{:S(2)}) collective-permute-start(bf16[256,128]{1,0:T(8,128)(2,1)S(1)} %collective-permute-done.12), channel_id=1, source_target_pairs={{8,0},{16,8},{24,16},{32,24},{40,32},{48,40},{56,48},{64,56},{72,6... | collective-permute-start | bytes 196616 | tf_op jit(solution)/shard_map/ppermute | solution.py:36
  95.1 7.8 %collective-permute-start.7 = (bf16[256,128]{1,0:T(8,128)(2,1)S(1)}, bf16[256,128]{1,0:T(8,128)(2,1)S(1)}, u32[]{:S(2)}, u32[]{:S(2)}) collective-permute-start(bf16[256,128]{1,0:T(8,128)(2,1)S(1)} %collective-permute-done.6), channel_id=1, source_target_pairs={{0,8},{8,16},{16,24},{24,32},{32,40},{40,48},{48,56},{56,64},{64,7... | collective-permute-start | bytes 196616 | tf_op jit(solution)/shard_map/ppermute | solution.py:34
  97.0 86.0 %collective-permute-start.14 = (bf16[256,128]{1,0:T(8,128)(2,1)}, bf16[256,128]{1,0:T(8,128)(2,1)}, u32[]{:S(2)}, u32[]{:S(2)}) collective-permute-start(bf16[256,128]{1,0:T(8,128)(2,1)} %collective-permute-done.13), channel_id=1, source_target_pairs={{8,0},{16,8},{24,16},{32,24},{40,32},{48,40},{56,48},{64,56},{72,6... | collective-permute-start | bytes 196616 | tf_op jit(solution)/shard_map/ppermute | solution.py:36
  111.5 132.4 %reduce-scatter.10.cloned.1.call-start = ((), (), s32[]{:S(2)}) async-start(), calls=%async_computation.8 | async-start | bytes 1114112
  171.4 149.4 %reduce-scatter.8.cloned.1.call-start = ((), (), s32[]{:S(2)}) async-start(), calls=%async_computation.6 | async-start | bytes 2228224 | tf_op jit(solution)/shard_map/reduce_scatter | solution.py:174
  179.6 203.9 %all-reduce.3.cloned.1.call-start = ((), (), s32[]{:S(2)}) async-start(), calls=%async_computation.7 | async-start | bytes 1048576 | tf_op jit(solution)/shard_map/psum | solution.py:217
  194.4 189.1 %copy-start.2 = (bf16[128,2048]{1,0:T(8,128)(2,1)S(1)}, bf16[128,2048]{1,0:T(8,128)(2,1)}, u32[]{:S(2)}) copy-start(bf16[128,2048]{1,0:T(8,128)(2,1)} %param.11) | copy-start | bytes 1572868
  (11 other events, 102.9 us)
Sparse Core Ops, SparseCore 0:
  32.1 76.7 reduce-scatter.5
  111.6 42.0 all-gather.1
  171.5 72.3 reduce-scatter.9
  247.0 73.7 reduce-scatter.7
  323.7 59.6 all-reduce.2
